TPU v7x, 32 devices: a whole 2x2x4 slice. The times are simulated.
32 devices in a mesh: grp: 2 (over x), seq: 16 (over z, y, core).
Axes of the slice: x: 2, y: 2, z: 4, core: 2. Of those that a mesh axis runs over, the one named last changes fastest.
Arguments:
- feats: bfloat16 [32, 128, 384], P('seq', None, 'grp'), may hold values from -6 to 6
- conv_weight: bfloat16 [3, 128, 128], replicated, may hold values from -0.3125 to 0.3125
- conv_bias: float32 [128], replicated, may hold values from -3 to 3
- latent_projection_weight: bfloat16 [16, 128], replicated, may hold values from -0.75 to 0.75
- noise: bfloat16 [32, 16, 384], P('seq', None, 'grp'), may hold values from -6 to 6
- step_index: int32 [1], replicated, may hold values from 0 to 49
- hist: bfloat16 [128, 64], P('seq'), may hold values from -6 to 6
- hist_level: int32 [128], P('seq'), may hold values from 0 to 2
- hist_count: int32 [16], replicated, may hold values from 1 to 8, 96 in all
- w_in: bfloat16 [64, 3072], replicated, may hold values from -2 to 2
- w_hist: bfloat16 [3, 64, 3072], replicated, may hold values from -0.75 to 0.75
- norm_gain: float32 [3072], replicated, may hold values from 0.5 to 2
- w_query: bfloat16 [3072, 1536], P(None, 'grp'), may hold values from -2 to 2
- w_key: bfloat16 [3072, 1536], P(None, 'grp'), may hold values from -2 to 2
- w_value: bfloat16 [3072, 1536], P(None, 'grp'), may hold values from -0.109375 to 0.109375
- q_gain: float32 [128], replicated, may hold values from 0.5 to 6
- k_gain: float32 [128], replicated, may hold values from 0.5 to 6
- w_out: bfloat16 [1536, 3072], P('grp'), may hold values from -0.5 to 0.5
Outputs:
- attention_out: bfloat16 [3072, 3072], P('seq', 'grp')
Inputs may be any that keep to these rules, and one draw needn't show every extreme that they name: hist_count[s] of the 8 history slots of seq index s are live; the largest count is exactly 8.
All inputs are finite; a program needn't handle non-finite values.
Results may differ from a plain program's by a relative error of at most 0.0095.
The roundings to bfloat16 on the way count: a program that leaves them out, or rounds other values in their place, can miss the bound.
Values may be sent and summed in bfloat16 or wider, within the bound.
No kernel may reach another device: no remote copies, remote signals or barrier semaphores. Data moves between devices by JAX's collectives and lax.ppermute only.
A program may use at most 256 MiB of HBM per device.

v0:
```python
import math
import jax
import jax.numpy as jnp
from jax import lax
from jax.sharding import PartitionSpec as P

STEPS = 50
EPSILON = 1e-06


def from_behind(value, axis, steps):
    count = lax.axis_size(axis)
    initial, last = (max(0, -steps), min(count, count - steps))
    return lax.ppermute(value, axis, [(source, source + steps) for source in range(initial, last)])


def time_embed(step_index, width):
    half_width = width // 2
    frequency = jnp.exp(-math.log(10000.0) * jnp.arange(half_width, dtype=jnp.float32) / half_width)
    angles = step_index[0].astype(jnp.float32) * frequency
    return jnp.concatenate([jnp.cos(angles), jnp.sin(angles)])


def rms_scale(values, gain):
    return values * lax.rsqrt(jnp.mean(values * values, axis=-1, keepdims=True) + EPSILON) * gain


def local(
    feats,
    conv_weight,
    conv_bias,
    latent_projection_weight,
    noise,
    step_index,
    hist,
    hist_level,
    hist_count,
    w_in,
    w_hist,
    norm_gain,
    w_query,
    w_key,
    w_value,
    q_gain,
    k_gain,
    w_out,
):
    frame_count, channels, pixels = feats.shape
    earlier = from_behind(feats, "seq", 1)
    padded = jnp.concatenate([earlier, feats], axis=0)
    total = jnp.zeros(feats.shape, jnp.float32)
    for tap_index in range(3):
        window = padded[2 - tap_index : 2 - tap_index + frame_count]
        total = total + jnp.einsum(
            "oc,tcp->top", conv_weight[tap_index], window, preferred_element_type=jnp.float32
        )
    hidden_state = jax.nn.silu(total + conv_bias[None, :, None]).astype(jnp.bfloat16)
    sigma = (STEPS - step_index[0].astype(jnp.float32)) / STEPS
    latent_input = jnp.einsum(
        "qb,zby->zqy", latent_projection_weight, hidden_state, preferred_element_type=jnp.float32
    )
    noisy = ((1.0 - sigma) * latent_input + sigma * noise.astype(jnp.float32)).astype(jnp.bfloat16)
    lat_channels = noisy.shape[1]
    patches = (
        noisy.reshape(frame_count, lat_channels, pixels // 4, 4)
        .transpose(0, 2, 1, 3)
        .reshape(frame_count, pixels // 4, lat_channels * 4)
    )
    width = w_in.shape[1]
    embed = time_embed(step_index, width)
    all_patches = lax.all_gather(patches, "grp", axis=1, tiled=True)
    block_rows = all_patches.shape[1]
    summed = (
        jnp.dot(
            all_patches.reshape(-1, all_patches.shape[2]), w_in, preferred_element_type=jnp.float32
        )
        + embed
    )
    tokens = (
        rms_scale(summed, norm_gain)
        .astype(jnp.bfloat16)
        .reshape(frame_count, block_rows, width)
        .reshape(-1, width)
    )
    history = jnp.zeros((hist.shape[0], width), jnp.float32)
    for level in range(3):
        history = (
            history
            + jnp.dot(hist, w_hist[level], preferred_element_type=jnp.float32)
            * (hist_level == level).astype(jnp.float32)[:, None]
        )
    history = rms_scale(history, norm_gain).astype(jnp.bfloat16)
    both_rows = jnp.concatenate([tokens, history], axis=0)
    sec_rows = tokens.shape[0]
    key_rows = both_rows.shape[0]
    head_size = q_gain.shape[0]
    heads_local = w_query.shape[1] // head_size
    query = rms_scale(
        jnp.dot(tokens, w_query, preferred_element_type=jnp.float32).reshape(
            sec_rows, heads_local, head_size
        ),
        q_gain,
    ).astype(jnp.bfloat16)
    flattened_keys = (
        rms_scale(
            jnp.dot(both_rows, w_key, preferred_element_type=jnp.float32).reshape(
                key_rows, heads_local, head_size
            ),
            k_gain,
        )
        .astype(jnp.bfloat16)
        .reshape(key_rows, heads_local * head_size)
    )
    values_flat = jnp.dot(both_rows, w_value, preferred_element_type=jnp.float32).astype(
        jnp.bfloat16
    )
    seq_count = lax.axis_size("seq")
    shard_ids = jnp.arange(seq_count, dtype=jnp.int32)
    scale = 1.0 / math.sqrt(head_size)
    run_max = jnp.full((heads_local, sec_rows), -1e30, jnp.float32)
    key_piece = lax.all_gather(flattened_keys, "seq", axis=0, tiled=True)
    value_piece = lax.all_gather(values_flat, "seq", axis=0, tiled=True)
    count_rows = key_piece.shape[0]
    row_index = jnp.arange(count_rows, dtype=jnp.int32)
    owner = row_index // key_rows
    local_index = row_index - owner * key_rows
    owner_count = jnp.sum(
        jnp.where(owner[:, None] == shard_ids[None, :], hist_count[None, :], 0), axis=1
    )
    alive = (local_index < sec_rows) | (local_index - sec_rows < owner_count)
    key_heads = key_piece.reshape(count_rows, heads_local, head_size)
    value_heads = value_piece.reshape(count_rows, heads_local, head_size)
    scores = (
        jnp.einsum("qhd,khd->hqk", query, key_heads, preferred_element_type=jnp.float32) * scale
    )
    scores = jnp.where(alive[None, None, :], scores, -1e30)
    new_max = jnp.maximum(run_max, jnp.max(scores, axis=-1))
    soft = jnp.where(alive[None, None, :], jnp.exp(scores - new_max[..., None]), 0.0)
    new_sum = jnp.sum(soft, axis=-1)
    new_weighted = jnp.einsum(
        "hqk,khd->hqd", soft.astype(jnp.bfloat16), value_heads, preferred_element_type=jnp.float32
    )
    attended = new_weighted / new_sum[..., None]
    heads_out = (
        attended.astype(jnp.bfloat16).transpose(1, 0, 2).reshape(sec_rows, heads_local * head_size)
    )
    partial_out = jnp.dot(heads_out, w_out, preferred_element_type=jnp.float32)
    return lax.psum_scatter(
        partial_out.astype(jnp.bfloat16), "grp", scatter_dimension=1, tiled=True
    )


def solution(mesh):
    placed = (
        P("seq", None, "grp"),
        P(),
        P(),
        P(),
        P("seq", None, "grp"),
        P(),
        P("seq", None),
        P("seq"),
        P(),
        P(),
        P(),
        P(),
        P(None, "grp"),
        P(None, "grp"),
        P(None, "grp"),
        P(),
        P(),
        P("grp", None),
    )
    return jax.shard_map(
        local, mesh=mesh, in_specs=placed, out_specs=P("seq", "grp"), check_vma=False
    )
```

profile of v0, /device:TPU:0, one launch (start us, length us, event | category | flops | bytes accessed | tf_op | source)
XLA Modules:
  0.0 191.2 jit_solution(1770931649743177877)
XLA Ops:
  6.5 2.5 %collective-permute-start = (bf16[2,128,192]{1,2,0:T(8,128)(2,1)}, bf16[2,128,192]{1,2,0:T(8,128)(2,1)S(1)}, u32[]{:S(2)}, u32[]{:S(2)}) collective-permute-start(bf16[2,128,192]{1,2,0:T(8,128)(2,1)} %param.18), channel_id=1, source_target_pairs={{0,1},{1,2},{2,3},{3,4},{4,5},{5,6},{6,7},{7,8},{8,9},{9,10},{10,1... | collective-permute-start | bytes 294920 | tf_op jit(solution)/shard_map/ppermute | solution.py:14
  9.8 1.1 fusion.46
  10.9 0.7 compare_convert_fusion
  11.5 1.2 convolution_multiply_fusion.2
  12.7 1.2 fusion.7
  13.9 1.3 multiply_reduce_fusion.2
  15.2 0.7 broadcast_bitcast_fusion
  15.9 0.8 multiply_convert_fusion.3
  16.7 1.0 convolution_add_fusion.2
  17.7 1.1 fusion.15
  19.1 4.8 %all_gather.9 = bf16[2,96,64]{2,0,1:T(2,128)(2,1)S(1)} all-gather(bf16[2,48,64]{2,0,1:T(2,128)(2,1)S(1)} %copy.73), channel_id=1, replica_groups=mesh['grp'=2,'seq'=16] {'grp'}, dimensions={1}, use_global_device_ids=true | all-gather | bytes 36864 | tf_op jit(solution)/shard_map/all_gather | solution.py:71
  24.1 0.6 multiply_reduce_fusion
  24.7 0.3 multiply_convert_fusion
  25.1 1.4 copy-done.5
  26.5 2.0 %fusion.66 = (f32[200,768]{1,0:T(8,128)}, f32[200,768]{1,0:T(8,128)S(1)}) fusion(bf16[3072,768]{1,0:T(8,128)(2,1)S(1)} %copy-done.5, bf16[8,3072]{1,0:T(8,128)(2,1)S(1)} %multiply_convert_fusion.3, bf16[192,3072]{1,0:T(8,128)(2,1)S(1)} %multiply_convert_fusion), kind=kOutput, calls=%fused_computation.94 | convolution fusion | flops 946329600 | bytes 7176192 | tf_op jit(solution)/shard_map/dot_general | solution.py:106
  28.5 1.2 mul.185
  29.7 0.3 reduce_sum.58
  30.2 0.3 mul.186
  30.5 0.9 fusion.27
  31.4 4.2 %convolution_convert_fusion.1 = bf16[200,768]{1,0:T(8,128)(2,1)} fusion(bf16[3072,768]{1,0:T(8,128)(2,1)} %param.32, bf16[8,3072]{1,0:T(8,128)(2,1)S(1)} %multiply_convert_fusion.3, bf16[192,3072]{1,0:T(8,128)(2,1)S(1)} %multiply_convert_fusion), kind=kOutput, calls=%fused_computation.18 | convolution fusion | flops 946329600 | bytes 6254592 | tf_op jit(solution)/shard_map/dot_general | solution.py:114
  35.9 3.4 %fusion.67 = f32[192,768]{1,0:T(8,128)S(1)} fusion(bf16[192,3072]{1,0:T(8,128)(2,1)S(1)} %multiply_convert_fusion, bf16[3072,768]{1,0:T(8,128)(2,1)} %param.30), kind=kOutput, calls=%fused_computation.95 | convolution fusion | flops 905969664 | bytes 6488064 | tf_op jit(solution)/shard_map/dot_general | solution.py:99
  39.4 0.3 multiply_reduce_fusion.1
  39.9 0.3 multiply_convert_fusion.1
  40.2 47.4 %all-gather.3.cloned.1.call-done = bf16[3200,768]{1,0:T(8,128)(2,1)} async-done(((bf16[200,768]{1,0:T(8,128)(2,1)}), bf16[3200,768]{1,0:T(8,128)(2,1)}) %all-gather.3.cloned.1.call-update) | async-done | bytes 4915216 | tf_op jit(solution)/shard_map/all_gather | solution.py:121
  87.6 7.4 %copy.79 = bf16[3200,768]{0,1:T(8,128)(2,1)} copy(bf16[3200,768]{1,0:T(8,128)(2,1)} %all-gather.3.cloned.1.call-done) | data formatting | bytes 9830400 | tf_op jit(solution)/shard_map/all_gather | solution.py:121
  95.1 10.4 %fusion = (f32[6,192]{1,0:T(8,128)S(1)}, f32[6,192,3200]{2,1,0:T(8,128)}) fusion(pred[3200]{0:T(1024)(128)(4,1)S(1)} %fusion.54, bf16[3200,6,128]{0,2,1:T(8,128)(2,1)} %bitcast.85, bf16[192,6,128]{2,1,0:T(8,128)(2,1)S(1)} %multiply_convert_fusion.1), kind=kOutput, calls=%fused_computation.2 | convolution fusion | flops 954776448 | bytes 19963520 | tf_op jit(solution)/shard_map/qhd,khd->hqk/dot_general | solution.py:134
  105.4 9.1 %fusion.1 = f32[6,192]{1,0:T(8,128)S(1)} fusion(f32[6,192,3200]{2,1,0:T(8,128)} %get-tuple-element.15, f32[6,192]{1,0:T(8,128)S(1)} %broadcast_maximum_fusion, pred[3200]{0:T(1024)(128)(4,1)S(1)} %fusion.54), kind=kLoop, calls=%fused_computation.3 | loop fusion | flops 18430848 | bytes 14758016 | tf_op jit(solution)/shard_map/reduce_sum | solution.py:139
  114.5 28.0 %all-gather.5.cloned.1.call-done = bf16[3200,768]{1,0:T(8,128)(2,1)} async-done(((bf16[200,768]{1,0:T(8,128)(2,1)}), bf16[3200,768]{1,0:T(8,128)(2,1)}) %all-gather.5.cloned.1.call-update) | async-done | bytes 4915216 | tf_op jit(solution)/shard_map/all_gather | solution.py:122
  142.5 7.4 %copy.82 = bf16[3200,768]{0,1:T(8,128)(2,1)} copy(bf16[3200,768]{1,0:T(8,128)(2,1)} %all-gather.5.cloned.1.call-done) | data formatting | bytes 9830400 | tf_op jit(solution)/shard_map/all_gather | solution.py:122
  149.9 9.7 %fusion.22 = bf16[6,24,8,128]{3,2,1,0:T(8,128)(2,1)S(1)} fusion(bf16[3200,6,128]{0,2,1:T(8,128)(2,1)} %bitcast.86, f32[6,192,3200]{2,1,0:T(8,128)} %get-tuple-element.15, f32[6,192]{1,0:T(8,128)S(1)} %broadcast_maximum_fusion, pred[3200]{0:T(1024)(128)(4,1)S(1)} %fusion.54, f32[192,6]{0,1:T(8,128)S(1)} %bitcast.90), kind=kOutput, calls=%fused_computation.29 | convolution fusion | flops 962445312 | bytes 19968128 | tf_op jit(solution)/shard_map/hqk,khd->hqd/dot_general | solution.py:140
  159.6 4.4 %convolution_convert_fusion = bf16[192,3072]{1,0:T(8,128)(2,1)} fusion(bf16[768,3072]{1,0:T(8,128)(2,1)} %param.35, bf16[6,24,8,128]{3,2,1,0:T(8,128)(2,1)S(1)} %fusion.22), kind=kOutput, calls=%fused_computation.8 | convolution fusion | flops 906559488 | bytes 6193152 | tf_op jit(solution)/shard_map/dot_general | solution.py:147
  164.1 20.5 %reduce-scatter.2.cloned.1.call-done = bf16[192,1536]{1,0:T(8,128)(2,1)} async-done(((bf16[192,3072]{1,0:T(8,128)(2,1)}), bf16[192,1536]{1,0:T(8,128)(2,1)}) %reduce-scatter.2.cloned.1.call-update) | async-done | bytes 589840 | tf_op jit(solution)/shard_map/reduce_scatter | solution.py:148
  (38 shorter events, 1.5 us)
Async XLA Ops:
  6.5 17.6 %copy-start = (bf16[64,3072]{1,0:T(8,128)(2,1)S(1)}, bf16[64,3072]{1,0:T(8,128)(2,1)}, u32[]{:S(2)}) copy-start(bf16[64,3072]{1,0:T(8,128)(2,1)} %param.27) | copy-start | bytes 1179652
  6.5 18.2 %copy-start.2 = (f32[3072]{0:T(1024)S(1)}, f32[3072]{0:T(1024)}, u32[]{:S(2)}) copy-start(f32[3072]{0:T(1024)} %param.29) | copy-start | bytes 36868
  6.5 81.1 %all-gather.3.cloned.1.call-start = ((), (), s32[]{:S(2)}) async-start(), calls=%async_computation.1 | async-start | bytes 5222400 | tf_op jit(solution)/shard_map/all_gather | solution.py:121
  6.5 10.1 %collective-permute-start = (bf16[2,128,192]{1,2,0:T(8,128)(2,1)}, bf16[2,128,192]{1,2,0:T(8,128)(2,1)S(1)}, u32[]{:S(2)}, u32[]{:S(2)}) collective-permute-start(bf16[2,128,192]{1,2,0:T(8,128)(2,1)} %param.18), channel_id=1, source_target_pairs={{0,1},{1,2},{2,3},{3,4},{4,5},{5,6},{6,7},{7,8},{8,9},{9,10},{10,1... | collective-permute-start | bytes 294920 | tf_op jit(solution)/shard_map/ppermute | solution.py:14
  24.1 2.3 %copy-start.5 = (bf16[3072,768]{1,0:T(8,128)(2,1)S(1)}, bf16[3072,768]{1,0:T(8,128)(2,1)}, u32[]{:S(2)}) copy-start(bf16[3072,768]{1,0:T(8,128)(2,1)} %param.31) | copy-start | bytes 14155780
  30.5 5.3 %copy-start.3 = (s32[16]{0:T(128)S(1)}, s32[16]{0:T(128)}, u32[]{:S(2)}) copy-start(s32[16]{0:T(128)} %param.26) | copy-start | bytes 196
  31.4 111.1 %all-gather.5.cloned.1.call-start = ((), (), s32[]{:S(2)}) async-start(), calls=%async_computation.2 | async-start | bytes 5222400 | tf_op jit(solution)/shard_map/all_gather | solution.py:122
  35.6 4.3 %copy-start.4 = (f32[128]{0:T(128)S(1)}, f32[128]{0:T(128)}, u32[]{:S(2)}) copy-start(f32[128]{0:T(128)} %param.33) | copy-start | bytes 1540
  35.7 149.0 %reduce-scatter.2.cloned.1.call-start = ((), (), s32[]{:S(2)}) async-start(), calls=%async_computation.3 | async-start | bytes 1769472 | tf_op jit(solution)/shard_map/reduce_scatter | solution.py:148
  149.9 34.7 %copy-start.1 = (bf16[64,3072]{1,0:T(8,128)(2,1)S(1)}, bf16[64,3072]{1,0:T(8,128)(2,1)}, u32[]{:S(2)}) copy-start(bf16[64,3072]{1,0:T(8,128)(2,1)} %param.27) | copy-start | bytes 1179652
Sparse Core Ops, SparseCore 0:
  31.5 56.0 all-gather.2
  89.8 52.6 all-gather.4
  164.2 20.3 reduce-scatter.1
where the time goes:
time: 192 us; the launch traced here: 191 us
  waiting for transfers between devices  96 us (50%)
  matrix products  41.5 us (22%)
  local copies, waits for them, and re-layouts  19.5 us (10%)
  between operations  14 us (7%)
  other arithmetic  12.8 us (7%)
  blocking collectives  4.77 us (2%)
  starting transfers between devices  2.61 us (1%)
    all_gather x1, waiting for transfers between devices, local(): key_piece = lax.all_gather(flattened_keys, 'seq', axis=0, tiled=True)  47.4 us
    all_gather x1, waiting for transfers between devices, local(): value_piece = lax.all_gather(values_flat, 'seq', axis=0, tiled=True)  28 us
    reduce_scatter x1, waiting for transfers between devices, local(): lax.psum_scatter(partial_out.astype(jnp.bfloat16), 'grp', scatter_dimensi...  20.5 us
    dot_general x1, matrix products, local(): jnp.einsum('qhd,khd->hqk', query, key_heads, preferred_element_type=jnp.f...  10.4 us
    dot_general x1, matrix products, local(): jnp.einsum('hqk,khd->hqd', soft.astype(jnp.bfloat16), value_heads, prefer...  9.68 us
    reduce_sum x1, other arithmetic, local(): new_sum = jnp.sum(soft, axis=-1)  9.09 us
    all_gather x1, local copies, waits for them, and re-layouts, local(): key_piece = lax.all_gather(flattened_keys, 'seq', axis=0, tiled=True)  7.44 us
    all_gather x1, local copies, waits for them, and re-layouts, local(): value_piece = lax.all_gather(values_flat, 'seq', axis=0, tiled=True)  7.44 us
  transfers between devices with their start and end apart: 4, of which 3 were waited for; matrix products, arithmetic and copies ran while one was open for 22% of the time, Pallas kernels for 0%

commit v1 on v0

--- a/solution.py
+++ b/solution.py
@@ -6,6 +6,16 @@
 
 STEPS = 50
 EPSILON = 1e-06
+
+
+def link_group(vals, join_dim):
+    vals = jnp.moveaxis(vals, 0, join_dim)
+    local_next = vals.shape
+    return vals.reshape(
+        *local_next[:join_dim],
+        local_next[join_dim] * local_next[join_dim + 1],
+        *local_next[join_dim + 2 :]
+    )
 
 
 def from_behind(value, axis, steps):
@@ -45,6 +55,34 @@
     k_gain,
     w_out,
 ):
+
+    def quotas_begin(array_in, axis_key, dim_k):
+        num = lax.axis_size(axis_key)
+        store = []
+        for jj in [*range(num)]:
+            store.append((jj, (jj + 1) % num))
+        found = []
+        for idx, w in store:
+            found.append((w, idx))
+        mid_arr, block_next = ([], [])
+        for k in tuple(range(num - 1)):
+            if k % 2 == 0:
+                mid_arr.append(
+                    lax.ppermute(
+                        mid_arr[-1] if mid_arr else array_in, axis_name=axis_key, perm=store
+                    )
+                )
+            else:
+                block_next.append(
+                    lax.ppermute(
+                        block_next[-1] if block_next else array_in, axis_name=axis_key, perm=found
+                    )
+                )
+        kept_arr = jnp.stack([*mid_arr[::-1], array_in, *block_next], 0)
+        value_now = lax.axis_index(axis_key) - len(mid_arr)
+        kept_arr = kept_arr[(jnp.arange(num) - value_now) % num]
+        return link_group(kept_arr, dim_k)
+
     frame_count, channels, pixels = feats.shape
     earlier = from_behind(feats, "seq", 1)
     padded = jnp.concatenate([earlier, feats], axis=0)
@@ -119,7 +157,7 @@
     scale = 1.0 / math.sqrt(head_size)
     run_max = jnp.full((heads_local, sec_rows), -1e30, jnp.float32)
     key_piece = lax.all_gather(flattened_keys, "seq", axis=0, tiled=True)
-    value_piece = lax.all_gather(values_flat, "seq", axis=0, tiled=True)
+    value_piece = quotas_begin(values_flat, "seq", dim_k=0)
     count_rows = key_piece.shape[0]
     row_index = jnp.arange(count_rows, dtype=jnp.int32)
     owner = row_index // key_rows

time: 192 us -> 227 us (1.18)
  starting transfers between devices: 2.61 us -> 35.9 us
  local copies, waits for them, and re-layouts: 19.5 us -> 49.4 us
  waiting for transfers between devices: 96 us -> 68.6 us
    ppermute x0 -> x15, waiting for transfers between devices: none -> 49.3 us  [the longest x8 37.2 us: quotas_begin(): lax.ppermute(mid_arr[-1] if mid_arr else array_in, axis_name=axis_key, pe...]
    all_gather x1, waiting for transfers between devices: 47.4 us -> 0.01 us  [local(): key_piece = lax.all_gather(flattened_keys, 'seq', axis=0, tiled=True)]
    ppermute x0 -> x15, starting transfers between devices: none -> 33.4 us  [the longest x7 32 us: quotas_begin(): lax.ppermute(block_next[-1] if block_next else array_in, axis_name=axis_k...]
    all_gather x1 -> x0, waiting for transfers between devices: 28 us -> none  [local(): value_piece = lax.all_gather(values_flat, 'seq', axis=0, tiled=True)]
    unnamed x12 -> x43, local copies, waits for them, and re-layouts: 1.41 us -> 21.3 us
    another operation x0 -> x2, local copies, waits for them, and re-layouts: none -> 12 us  [the longest x1 11.2 us: local(): value_heads = value_piece.reshape(count_rows, heads_local, head_size)]
    all_gather x1 -> x0, local copies, waits for them, and re-layouts: 7.44 us -> none  [local(): value_piece = lax.all_gather(values_flat, 'seq', axis=0, tiled=True)]
    gather x0 -> x1, local copies, waits for them, and re-layouts: none -> 5.55 us  [quotas_begin(): kept_arr = kept_arr[(jnp.arange(num) - value_now) % num]]
  transfers between devices with their start and end apart: 4 -> 18, of which waited for: 3 -> 13; matrix products, arithmetic and copies ran while one was open for 22% -> 23% of each run, Pallas kernels for 0% -> 0%
where the time goes in v1:
time: 227 us; the launch traced here: 226 us
  waiting for transfers between devices  68.6 us (30%)
  local copies, waits for them, and re-layouts  49.4 us (22%)
  matrix products  40 us (18%)
  starting transfers between devices  35.9 us (16%)
  between operations  14.4 us (6%)
  other arithmetic  13 us (6%)
  blocking collectives  4.76 us (2%)
    ppermute x8, waiting for transfers between devices, quotas_begin(): lax.ppermute(mid_arr[-1] if mid_arr else array_in, axis_name=axis_key, pe...  37.2 us
    ppermute x7, starting transfers between devices, quotas_begin(): lax.ppermute(block_next[-1] if block_next else array_in, axis_name=axis_k...  32 us
    unnamed x43, local copies, waits for them, and re-layouts  21.3 us
    reduce_scatter x1, waiting for transfers between devices, local(): lax.psum_scatter(partial_out.astype(jnp.bfloat16), 'grp', scatter_dimensi...  19.3 us
    ppermute x7, waiting for transfers between devices, quotas_begin(): lax.ppermute(block_next[-1] if block_next else array_in, axis_name=axis_k...  12 us
    dot_general x1, matrix products, local(): jnp.einsum('hqk,khd->hqd', soft.astype(jnp.bfloat16), value_heads, prefer...  11.3 us
    another operation x1, local copies, waits for them, and re-layouts, local(): value_heads = value_piece.reshape(count_rows, heads_local, head_size)  11.2 us
    dot_general x1, matrix products, local(): jnp.einsum('qhd,khd->hqk', query, key_heads, preferred_element_type=jnp.f...  10.2 us
  transfers between devices with their start and end apart: 18, of which 13 were waited for; matrix products, arithmetic and copies ran while one was open for 23% of the time, Pallas kernels for 0%

profile of v1, /device:TPU:0, one launch (start us, length us, event | category | flops | bytes accessed | tf_op | source)
XLA Modules:
  0.0 226.0 jit_solution(6816570353035609079)
XLA Ops:
  6.5 2.5 %collective-permute-start = (bf16[2,128,192]{1,2,0:T(8,128)(2,1)}, bf16[2,128,192]{1,2,0:T(8,128)(2,1)S(1)}, u32[]{:S(2)}, u32[]{:S(2)}) collective-permute-start(bf16[2,128,192]{1,2,0:T(8,128)(2,1)} %param.18), channel_id=1, source_target_pairs={{0,1},{1,2},{2,3},{3,4},{4,5},{5,6},{6,7},{7,8},{8,9},{9,10},{10,1... | collective-permute-start | bytes 294920 | tf_op jit(solution)/shard_map/ppermute | solution.py:24
  19.2 4.8 %all_gather.6 = bf16[2,96,64]{2,0,1:T(2,128)(2,1)S(1)} all-gather(bf16[2,48,64]{2,0,1:T(2,128)(2,1)S(1)} %copy.73), channel_id=1, replica_groups=mesh['grp'=2,'seq'=16] {'grp'}, dimensions={1}, use_global_device_ids=true | all-gather | bytes 36864 | tf_op jit(solution)/shard_map/all_gather | solution.py:109
  26.5 2.0 fusion.77
  31.4 3.5 %convolution_convert_fusion.1 = bf16[200,768]{1,0:T(8,128)(2,1)S(1)} fusion(bf16[3072,768]{1,0:T(8,128)(2,1)} %param.32, bf16[8,3072]{1,0:T(8,128)(2,1)S(1)} %multiply_convert_fusion.3, bf16[192,3072]{1,0:T(8,128)(2,1)S(1)} %multiply_convert_fusion), kind=kOutput, calls=%fused_computation.20 | convolution fusion | flops 946329600 | bytes 6254592 | tf_op jit(solution)/shard_map/dot_general | solution.py:152
  36.2 7.8 %collective-permute-done.1 = bf16[200,768]{1,0:T(8,128)(2,1)S(1)} collective-permute-done((bf16[200,768]{1,0:T(8,128)(2,1)S(1)}, bf16[200,768]{1,0:T(8,128)(2,1)S(1)}, u32[]{:S(2)}, u32[]{:S(2)}) %collective-permute-start.1) | collective-permute-done | bytes 307232 | tf_op jit(solution)/shard_map/ppermute | solution.py:71
  44.0 4.4 %collective-permute-start.9 = (bf16[200,768]{1,0:T(8,128)(2,1)S(1)}, bf16[200,768]{1,0:T(8,128)(2,1)S(1)}, u32[]{:S(2)}, u32[]{:S(2)}) collective-permute-start(bf16[200,768]{1,0:T(8,128)(2,1)S(1)} %convolution_convert_fusion.1), channel_id=1, source_target_pairs={{1,0},{2,1},{3,2},{4,3},{5,4},{6,5},{7,6},{8,7},{9,8},{10,9},{11,1... | collective-permute-start | bytes 921608 | tf_op jit(solution)/shard_map/ppermute | solution.py:77
  48.4 11.2 %collective-permute-done.2 = bf16[200,768]{1,0:T(8,128)(2,1)S(1)} collective-permute-done((bf16[200,768]{1,0:T(8,128)(2,1)S(1)}, bf16[200,768]{1,0:T(8,128)(2,1)S(1)}, u32[]{:S(2)}, u32[]{:S(2)}) %collective-permute-start.2) | collective-permute-done | bytes 307232 | tf_op jit(solution)/shard_map/ppermute | solution.py:71
  59.7 4.4 %collective-permute-start.10 = (bf16[200,768]{1,0:T(8,128)(2,1)S(1)}, bf16[200,768]{1,0:T(8,128)(2,1)S(1)}, u32[]{:S(2)}, u32[]{:S(2)}) collective-permute-start(bf16[200,768]{1,0:T(8,128)(2,1)S(1)} %collective-permute-done.9), channel_id=1, source_target_pairs={{1,0},{2,1},{3,2},{4,3},{5,4},{6,5},{7,6},{8,7},{9,8},{10,9},{11,1... | collective-permute-start | bytes 921608 | tf_op jit(solution)/shard_map/ppermute | solution.py:77
  64.1 5.7 %collective-permute-done.3 = bf16[200,768]{1,0:T(8,128)(2,1)S(1)} collective-permute-done((bf16[200,768]{1,0:T(8,128)(2,1)S(1)}, bf16[200,768]{1,0:T(8,128)(2,1)S(1)}, u32[]{:S(2)}, u32[]{:S(2)}) %collective-permute-start.3) | collective-permute-done | bytes 307232 | tf_op jit(solution)/shard_map/ppermute | solution.py:71
  69.8 5.1 %collective-permute-done.10 = bf16[200,768]{1,0:T(8,128)(2,1)S(1)} collective-permute-done((bf16[200,768]{1,0:T(8,128)(2,1)S(1)}, bf16[200,768]{1,0:T(8,128)(2,1)S(1)}, u32[]{:S(2)}, u32[]{:S(2)}) %collective-permute-start.10) | collective-permute-done | bytes 307232 | tf_op jit(solution)/shard_map/ppermute | solution.py:77
  74.9 4.6 %collective-permute-start.11 = (bf16[200,768]{1,0:T(8,128)(2,1)S(1)}, bf16[200,768]{1,0:T(8,128)(2,1)S(1)}, u32[]{:S(2)}, u32[]{:S(2)}) collective-permute-start(bf16[200,768]{1,0:T(8,128)(2,1)S(1)} %collective-permute-done.10), channel_id=1, source_target_pairs={{1,0},{2,1},{3,2},{4,3},{5,4},{6,5},{7,6},{8,7},{9,8},{10,9},{11,1... | collective-permute-start | bytes 921608 | tf_op jit(solution)/shard_map/ppermute | solution.py:77
  79.5 3.9 %collective-permute-done.4 = bf16[200,768]{1,0:T(8,128)(2,1)} collective-permute-done((bf16[200,768]{1,0:T(8,128)(2,1)S(1)}, bf16[200,768]{1,0:T(8,128)(2,1)}, u32[]{:S(2)}, u32[]{:S(2)}) %collective-permute-start.4) | collective-permute-done | bytes 307232 | tf_op jit(solution)/shard_map/ppermute | solution.py:71
  83.6 1.9 collective-permute-done.11
  85.5 4.6 %collective-permute-start.12 = (bf16[200,768]{1,0:T(8,128)(2,1)S(1)}, bf16[200,768]{1,0:T(8,128)(2,1)}, u32[]{:S(2)}, u32[]{:S(2)}) collective-permute-start(bf16[200,768]{1,0:T(8,128)(2,1)S(1)} %collective-permute-done.11), channel_id=1, source_target_pairs={{1,0},{2,1},{3,2},{4,3},{5,4},{6,5},{7,6},{8,7},{9,8},{10,9},{11,1... | collective-permute-start | bytes 921608 | tf_op jit(solution)/shard_map/ppermute | solution.py:77
  90.1 2.6 %collective-permute-done.5 = bf16[200,768]{1,0:T(8,128)(2,1)S(1)} collective-permute-done((bf16[200,768]{1,0:T(8,128)(2,1)}, bf16[200,768]{1,0:T(8,128)(2,1)S(1)}, u32[]{:S(2)}, u32[]{:S(2)}) %collective-permute-start.5) | collective-permute-done | bytes 307232 | tf_op jit(solution)/shard_map/ppermute | solution.py:71
  92.8 1.8 collective-permute-done.12
  94.5 4.9 %collective-permute-start.13 = (bf16[200,768]{1,0:T(8,128)(2,1)}, bf16[200,768]{1,0:T(8,128)(2,1)}, u32[]{:S(2)}, u32[]{:S(2)}) collective-permute-start(bf16[200,768]{1,0:T(8,128)(2,1)} %collective-permute-done.12), channel_id=1, source_target_pairs={{1,0},{2,1},{3,2},{4,3},{5,4},{6,5},{7,6},{8,7},{9,8},{10,9},{11,1... | collective-permute-start | bytes 921608 | tf_op jit(solution)/shard_map/ppermute | solution.py:77
  99.4 3.9 %collective-permute-done.6 = bf16[200,768]{1,0:T(8,128)(2,1)} collective-permute-done((bf16[200,768]{1,0:T(8,128)(2,1)S(1)}, bf16[200,768]{1,0:T(8,128)(2,1)}, u32[]{:S(2)}, u32[]{:S(2)}) %collective-permute-start.6) | collective-permute-done | bytes 307232 | tf_op jit(solution)/shard_map/ppermute | solution.py:71
  103.4 3.4 %fusion.78 = f32[192,768]{1,0:T(8,128)S(1)} fusion(bf16[192,3072]{1,0:T(8,128)(2,1)S(1)} %multiply_convert_fusion, bf16[3072,768]{1,0:T(8,128)(2,1)} %param.30), kind=kOutput, calls=%fused_computation.120 | convolution fusion | flops 905969664 | bytes 6488064 | tf_op jit(solution)/shard_map/dot_general | solution.py:137
  107.3 4.4 %collective-permute-start.14 = (bf16[200,768]{1,0:T(8,128)(2,1)}, bf16[200,768]{1,0:T(8,128)(2,1)}, u32[]{:S(2)}, u32[]{:S(2)}) collective-permute-start(bf16[200,768]{1,0:T(8,128)(2,1)} %collective-permute-done.13), channel_id=1, source_target_pairs={{1,0},{2,1},{3,2},{4,3},{5,4},{6,5},{7,6},{8,7},{9,8},{10,9},{11,1... | collective-permute-start | bytes 921608 | tf_op jit(solution)/shard_map/ppermute | solution.py:77
  113.2 3.2 %collective-permute-done.14 = bf16[200,768]{1,0:T(8,128)(2,1)} collective-permute-done((bf16[200,768]{1,0:T(8,128)(2,1)}, bf16[200,768]{1,0:T(8,128)(2,1)}, u32[]{:S(2)}, u32[]{:S(2)}) %collective-permute-start.14) | collective-permute-done | bytes 307232 | tf_op jit(solution)/shard_map/ppermute | solution.py:77
  116.4 4.6 %collective-permute-start.15 = (bf16[200,768]{1,0:T(8,128)(2,1)}, bf16[200,768]{1,0:T(8,128)(2,1)S(1)}, u32[]{:S(2)}, u32[]{:S(2)}) collective-permute-start(bf16[200,768]{1,0:T(8,128)(2,1)} %collective-permute-done.14), channel_id=1, source_target_pairs={{1,0},{2,1},{3,2},{4,3},{5,4},{6,5},{7,6},{8,7},{9,8},{10,9},{11,1... | collective-permute-start | bytes 921608 | tf_op jit(solution)/shard_map/ppermute | solution.py:77
  135.1 1.7 bitcast_dynamic-update-slice_fusion.4
  138.6 1.7 bitcast_dynamic-update-slice_fusion.2
  142.8 5.6 %gather_fusion = bf16[16,200,768]{2,1,0:T(8,128)(2,1)} fusion(bf16[16,200,768]{2,1,0:T(8,128)(2,1)} %bitcast_dynamic-update-slice_fusion, s32[1024]{0:T(1024)S(1)} %pad_clamp_fusion), kind=kCustom, calls=%fused_computation | custom fusion | bytes 9830464 | tf_op jit(solution)/shard_map/gather | solution.py:83
  148.3 11.2 %reshape.171 = bf16[3200,6,128]{2,1,0:T(8,128)(2,1)} reshape(bf16[16,200,768]{2,1,0:T(8,128)(2,1)} %gather_fusion) | data formatting | bytes 9830400 | tf_op jit(solution)/shard_map/reshape;reshape | solution.py:170
  159.5 7.4 %copy.79 = bf16[3200,768]{0,1:T(8,128)(2,1)} copy(bf16[3200,768]{1,0:T(8,128)(2,1)} %all-gather.2.cloned.1.call-done) | data formatting | bytes 9830400 | tf_op jit(solution)/shard_map/all_gather | solution.py:159
  167.0 10.2 %fusion = (f32[6,192]{1,0:T(8,128)S(1)}, f32[6,192,3200]{2,1,0:T(8,128)}) fusion(pred[3200]{0:T(1024)(128)(4,1)S(1)} %fusion.63, bf16[3200,6,128]{0,2,1:T(8,128)(2,1)} %bitcast.117, bf16[192,6,128]{2,1,0:T(8,128)(2,1)S(1)} %multiply_convert_fusion.1), kind=kOutput, calls=%fused_computation.3 | convolution fusion | flops 954776448 | bytes 19963520 | tf_op jit(solution)/shard_map/qhd,khd->hqk/dot_general | solution.py:172
  177.1 9.2 %fusion.1 = f32[6,192]{1,0:T(8,128)S(1)} fusion(f32[6,192,3200]{2,1,0:T(8,128)} %get-tuple-element.15, f32[6,192]{1,0:T(8,128)S(1)} %broadcast_maximum_fusion, pred[3200]{0:T(1024)(128)(4,1)S(1)} %fusion.63), kind=kLoop, calls=%fused_computation.4 | loop fusion | flops 18430848 | bytes 14758016 | tf_op jit(solution)/shard_map/reduce_sum | solution.py:177
  186.3 11.3 %fusion.29 = bf16[6,24,8,128]{3,2,1,0:T(8,128)(2,1)S(1)} fusion(bf16[3200,6,128]{2,1,0:T(8,128)(2,1)} %reshape.171, f32[6,192,3200]{2,1,0:T(8,128)} %get-tuple-element.15, f32[6,192]{1,0:T(8,128)S(1)} %broadcast_maximum_fusion, pred[3200]{0:T(1024)(128)(4,1)S(1)} %fusion.63, f32[192,6]{0,1:T(8,128)S(1)} %bitcast.123), kind=kOutput, calls=%fused_computation.31 | convolution fusion | flops 962445312 | bytes 19968128 | tf_op jit(solution)/shard_map/hqk,khd->hqd/dot_general | solution.py:178
  197.7 2.1 convolution_convert_fusion
  199.9 19.3 %reduce-scatter.2.cloned.1.call-done = bf16[192,1536]{1,0:T(8,128)(2,1)} async-done(((bf16[192,3072]{1,0:T(8,128)(2,1)}), bf16[192,1536]{1,0:T(8,128)(2,1)}) %reduce-scatter.2.cloned.1.call-update) | async-done | bytes 589840 | tf_op jit(solution)/shard_map/reduce_scatter | solution.py:186
  (101 shorter events, 36.5 us)
Async XLA Ops:
  6.5 17.6 %copy-start = (bf16[64,3072]{1,0:T(8,128)(2,1)S(1)}, bf16[64,3072]{1,0:T(8,128)(2,1)}, u32[]{:S(2)}) copy-start(bf16[64,3072]{1,0:T(8,128)(2,1)} %param.27) | copy-start | bytes 1179652
  6.5 18.2 %copy-start.8 = (f32[3072]{0:T(1024)S(1)}, f32[3072]{0:T(1024)}, u32[]{:S(2)}) copy-start(f32[3072]{0:T(1024)} %param.29) | copy-start | bytes 36868
  6.5 153.0 %all-gather.2.cloned.1.call-start = ((), (), s32[]{:S(2)}) async-start(), calls=%async_computation.1 | async-start | bytes 5222400 | tf_op jit(solution)/shard_map/all_gather | solution.py:159
  6.5 10.1 %collective-permute-start = (bf16[2,128,192]{1,2,0:T(8,128)(2,1)}, bf16[2,128,192]{1,2,0:T(8,128)(2,1)S(1)}, u32[]{:S(2)}, u32[]{:S(2)}) collective-permute-start(bf16[2,128,192]{1,2,0:T(8,128)(2,1)} %param.18), channel_id=1, source_target_pairs={{0,1},{1,2},{2,3},{3,4},{4,5},{5,6},{6,7},{7,8},{8,9},{9,10},{10,1... | collective-permute-start | bytes 294920 | tf_op jit(solution)/shard_map/ppermute | solution.py:24
  24.1 2.3 %copy-start.11 = (bf16[3072,768]{1,0:T(8,128)(2,1)S(1)}, bf16[3072,768]{1,0:T(8,128)(2,1)}, u32[]{:S(2)}) copy-start(bf16[3072,768]{1,0:T(8,128)(2,1)} %param.31) | copy-start | bytes 14155780
  30.5 53.0 %copy-start.9 = (s32[16]{0:T(128)S(1)}, s32[16]{0:T(128)}, u32[]{:S(2)}) copy-start(s32[16]{0:T(128)} %param.26) | copy-start | bytes 196
  31.4 187.8 %reduce-scatter.2.cloned.1.call-start = ((), (), s32[]{:S(2)}) async-start(), calls=%async_computation.2 | async-start | bytes 1769472 | tf_op jit(solution)/shard_map/reduce_scatter | solution.py:186
  34.9 77.9 %copy-start.10 = (f32[128]{0:T(128)S(1)}, f32[128]{0:T(128)}, u32[]{:S(2)}) copy-start(f32[128]{0:T(128)} %param.33) | copy-start | bytes 1540
  34.9 9.0 %collective-permute-start.1 = (bf16[200,768]{1,0:T(8,128)(2,1)S(1)}, bf16[200,768]{1,0:T(8,128)(2,1)S(1)}, u32[]{:S(2)}, u32[]{:S(2)}) collective-permute-start(bf16[200,768]{1,0:T(8,128)(2,1)S(1)} %convolution_convert_fusion.1), channel_id=1, source_target_pairs={{0,1},{1,2},{2,3},{3,4},{4,5},{5,6},{6,7},{7,8},{8,9},{9,10},{10,1... | collective-permute-start | bytes 921608 | tf_op jit(solution)/shard_map/ppermute | solution.py:71
  44.0 15.7 %collective-permute-start.2 = (bf16[200,768]{1,0:T(8,128)(2,1)S(1)}, bf16[200,768]{1,0:T(8,128)(2,1)S(1)}, u32[]{:S(2)}, u32[]{:S(2)}) collective-permute-start(bf16[200,768]{1,0:T(8,128)(2,1)S(1)} %collective-permute-done.1), channel_id=1, source_target_pairs={{0,1},{1,2},{2,3},{3,4},{4,5},{5,6},{6,7},{7,8},{8,9},{9,10},{10,1... | collective-permute-start | bytes 921608 | tf_op jit(solution)/shard_map/ppermute | solution.py:71
  44.0 15.7 %collective-permute-start.9 = (bf16[200,768]{1,0:T(8,128)(2,1)S(1)}, bf16[200,768]{1,0:T(8,128)(2,1)S(1)}, u32[]{:S(2)}, u32[]{:S(2)}) collective-permute-start(bf16[200,768]{1,0:T(8,128)(2,1)S(1)} %convolution_convert_fusion.1), channel_id=1, source_target_pairs={{1,0},{2,1},{3,2},{4,3},{5,4},{6,5},{7,6},{8,7},{9,8},{10,9},{11,1... | collective-permute-start | bytes 921608 | tf_op jit(solution)/shard_map/ppermute | solution.py:77
  59.7 10.1 %collective-permute-start.3 = (bf16[200,768]{1,0:T(8,128)(2,1)S(1)}, bf16[200,768]{1,0:T(8,128)(2,1)S(1)}, u32[]{:S(2)}, u32[]{:S(2)}) collective-permute-start(bf16[200,768]{1,0:T(8,128)(2,1)S(1)} %collective-permute-done.2), channel_id=1, source_target_pairs={{0,1},{1,2},{2,3},{3,4},{4,5},{5,6},{6,7},{7,8},{8,9},{9,10},{10,1... | collective-permute-start | bytes 921608 | tf_op jit(solution)/shard_map/ppermute | solution.py:71
  59.7 15.2 %collective-permute-start.10 = (bf16[200,768]{1,0:T(8,128)(2,1)S(1)}, bf16[200,768]{1,0:T(8,128)(2,1)S(1)}, u32[]{:S(2)}, u32[]{:S(2)}) collective-permute-start(bf16[200,768]{1,0:T(8,128)(2,1)S(1)} %collective-permute-done.9), channel_id=1, source_target_pairs={{1,0},{2,1},{3,2},{4,3},{5,4},{6,5},{7,6},{8,7},{9,8},{10,9},{11,1... | collective-permute-start | bytes 921608 | tf_op jit(solution)/shard_map/ppermute | solution.py:77
  69.8 33.5 %copy-start.4 = (bf16[200,768]{1,0:T(8,128)(2,1)}, bf16[200,768]{1,0:T(8,128)(2,1)S(1)}, u32[]{:S(2)}) copy-start(bf16[200,768]{1,0:T(8,128)(2,1)S(1)} %collective-permute-done.3) | copy-start | bytes 921604
  69.8 13.7 %collective-permute-start.4 = (bf16[200,768]{1,0:T(8,128)(2,1)S(1)}, bf16[200,768]{1,0:T(8,128)(2,1)}, u32[]{:S(2)}, u32[]{:S(2)}) collective-permute-start(bf16[200,768]{1,0:T(8,128)(2,1)S(1)} %collective-permute-done.3), channel_id=1, source_target_pairs={{0,1},{1,2},{2,3},{3,4},{4,5},{5,6},{6,7},{7,8},{8,9},{9,10},{10,1... | collective-permute-start | bytes 921608 | tf_op jit(solution)/shard_map/ppermute | solution.py:71
  74.9 31.9 %copy-start.2 = (bf16[200,768]{1,0:T(8,128)(2,1)}, bf16[200,768]{1,0:T(8,128)(2,1)S(1)}, u32[]{:S(2)}) copy-start(bf16[200,768]{1,0:T(8,128)(2,1)S(1)} %collective-permute-done.10) | copy-start | bytes 921604
  74.9 10.6 %collective-permute-start.11 = (bf16[200,768]{1,0:T(8,128)(2,1)S(1)}, bf16[200,768]{1,0:T(8,128)(2,1)S(1)}, u32[]{:S(2)}, u32[]{:S(2)}) collective-permute-start(bf16[200,768]{1,0:T(8,128)(2,1)S(1)} %collective-permute-done.10), channel_id=1, source_target_pairs={{1,0},{2,1},{3,2},{4,3},{5,4},{6,5},{7,6},{8,7},{9,8},{10,9},{11,1... | collective-permute-start | bytes 921608 | tf_op jit(solution)/shard_map/ppermute | solution.py:77
  83.4 9.3 %collective-permute-start.5 = (bf16[200,768]{1,0:T(8,128)(2,1)}, bf16[200,768]{1,0:T(8,128)(2,1)S(1)}, u32[]{:S(2)}, u32[]{:S(2)}) collective-permute-start(bf16[200,768]{1,0:T(8,128)(2,1)} %collective-permute-done.4), channel_id=1, source_target_pairs={{0,1},{1,2},{2,3},{3,4},{4,5},{5,6},{6,7},{7,8},{8,9},{9,10},{10,1... | collective-permute-start | bytes 921608 | tf_op jit(solution)/shard_map/ppermute | solution.py:71
  85.5 17.8 %copy-start.6 = (bf16[200,768]{1,0:T(8,128)(2,1)}, bf16[200,768]{1,0:T(8,128)(2,1)S(1)}, u32[]{:S(2)}) copy-start(bf16[200,768]{1,0:T(8,128)(2,1)S(1)} %collective-permute-done.11) | copy-start | bytes 921604
  85.5 9.0 %collective-permute-start.12 = (bf16[200,768]{1,0:T(8,128)(2,1)S(1)}, bf16[200,768]{1,0:T(8,128)(2,1)}, u32[]{:S(2)}, u32[]{:S(2)}) collective-permute-start(bf16[200,768]{1,0:T(8,128)(2,1)S(1)} %collective-permute-done.11), channel_id=1, source_target_pairs={{1,0},{2,1},{3,2},{4,3},{5,4},{6,5},{7,6},{8,7},{9,8},{10,9},{11,1... | collective-permute-start | bytes 921608 | tf_op jit(solution)/shard_map/ppermute | solution.py:77
  92.7 10.5 %copy-start.7 = (bf16[200,768]{1,0:T(8,128)(2,1)}, bf16[200,768]{1,0:T(8,128)(2,1)S(1)}, u32[]{:S(2)}) copy-start(bf16[200,768]{1,0:T(8,128)(2,1)S(1)} %collective-permute-done.5) | copy-start | bytes 921604
  92.7 10.5 %collective-permute-start.6 = (bf16[200,768]{1,0:T(8,128)(2,1)S(1)}, bf16[200,768]{1,0:T(8,128)(2,1)}, u32[]{:S(2)}, u32[]{:S(2)}) collective-permute-start(bf16[200,768]{1,0:T(8,128)(2,1)S(1)} %collective-permute-done.5), channel_id=1, source_target_pairs={{0,1},{1,2},{2,3},{3,4},{4,5},{5,6},{6,7},{7,8},{8,9},{9,10},{10,1... | collective-permute-start | bytes 921608 | tf_op jit(solution)/shard_map/ppermute | solution.py:71
  94.5 12.7 %collective-permute-start.13 = (bf16[200,768]{1,0:T(8,128)(2,1)}, bf16[200,768]{1,0:T(8,128)(2,1)}, u32[]{:S(2)}, u32[]{:S(2)}) collective-permute-start(bf16[200,768]{1,0:T(8,128)(2,1)} %collective-permute-done.12), channel_id=1, source_target_pairs={{1,0},{2,1},{3,2},{4,3},{5,4},{6,5},{7,6},{8,7},{9,8},{10,9},{11,1... | collective-permute-start | bytes 921608 | tf_op jit(solution)/shard_map/ppermute | solution.py:77
  103.3 9.4 %collective-permute-start.7 = (bf16[200,768]{1,0:T(8,128)(2,1)}, bf16[200,768]{1,0:T(8,128)(2,1)}, u32[]{:S(2)}, u32[]{:S(2)}) collective-permute-start(bf16[200,768]{1,0:T(8,128)(2,1)} %collective-permute-done.6), channel_id=1, source_target_pairs={{0,1},{1,2},{2,3},{3,4},{4,5},{5,6},{6,7},{7,8},{8,9},{9,10},{10,1... | collective-permute-start | bytes 921608 | tf_op jit(solution)/shard_map/ppermute | solution.py:71
  106.9 23.8 %copy-start.5 = (bf16[200,768]{1,0:T(8,128)(2,1)S(1)}, bf16[200,768]{1,0:T(8,128)(2,1)}, u32[]{:S(2)}) copy-start(bf16[200,768]{1,0:T(8,128)(2,1)} %copy-done.4) | copy-start | bytes 921604
  106.9 27.5 %copy-start.3 = (bf16[200,768]{1,0:T(8,128)(2,1)S(1)}, bf16[200,768]{1,0:T(8,128)(2,1)}, u32[]{:S(2)}) copy-start(bf16[200,768]{1,0:T(8,128)(2,1)} %copy-done.2) | copy-start | bytes 921604
  107.3 9.1 %collective-permute-start.14 = (bf16[200,768]{1,0:T(8,128)(2,1)}, bf16[200,768]{1,0:T(8,128)(2,1)}, u32[]{:S(2)}, u32[]{:S(2)}) collective-permute-start(bf16[200,768]{1,0:T(8,128)(2,1)} %collective-permute-done.13), channel_id=1, source_target_pairs={{1,0},{2,1},{3,2},{4,3},{5,4},{6,5},{7,6},{8,7},{9,8},{10,9},{11,1... | collective-permute-start | bytes 921608 | tf_op jit(solution)/shard_map/ppermute | solution.py:77
  112.7 9.4 %collective-permute-start.8 = (bf16[200,768]{1,0:T(8,128)(2,1)}, bf16[200,768]{1,0:T(8,128)(2,1)}, u32[]{:S(2)}, u32[]{:S(2)}) collective-permute-start(bf16[200,768]{1,0:T(8,128)(2,1)} %collective-permute-done.7), channel_id=1, source_target_pairs={{0,1},{1,2},{2,3},{3,4},{4,5},{5,6},{6,7},{7,8},{8,9},{9,10},{10,1... | collective-permute-start | bytes 921608 | tf_op jit(solution)/shard_map/ppermute | solution.py:71
  116.4 25.6 %collective-permute-start.15 = (bf16[200,768]{1,0:T(8,128)(2,1)}, bf16[200,768]{1,0:T(8,128)(2,1)S(1)}, u32[]{:S(2)}, u32[]{:S(2)}) collective-permute-start(bf16[200,768]{1,0:T(8,128)(2,1)} %collective-permute-done.14), channel_id=1, source_target_pairs={{1,0},{2,1},{3,2},{4,3},{5,4},{6,5},{7,6},{8,7},{9,8},{10,9},{11,1... | collective-permute-start | bytes 921608 | tf_op jit(solution)/shard_map/ppermute | solution.py:77
  177.1 20.6 %slice-start = ((s8[4718592]{0:T(1024)(128)(4,1)}), s8[4194304]{0:T(1024)(128)(4,1)S(1)}, s32[]{:S(2)}) async-start(s8[4718592]{0:T(1024)(128)(4,1)} %bitcast.118), calls=%async_computation.3 | async-start | bytes 8388608
  186.3 11.4 %slice-start.1 = ((s8[4718592]{0:T(1024)(128)(4,1)}), s8[524288]{0:T(1024)(128)(4,1)S(1)}, s32[]{:S(2)}) async-start(s8[4718592]{0:T(1024)(128)(4,1)} %bitcast.118), calls=%async_computation.4 | async-start | bytes 1048576
  186.3 32.8 %copy-start.1 = (bf16[64,3072]{1,0:T(8,128)(2,1)S(1)}, bf16[64,3072]{1,0:T(8,128)(2,1)}, u32[]{:S(2)}) copy-start(bf16[64,3072]{1,0:T(8,128)(2,1)} %param.27) | copy-start | bytes 1179652
Sparse Core Ops, SparseCore 0:
  31.5 71.5 all-gather.1
  200.0 19.1 reduce-scatter.1
